TPU v7x, 32 devices: a whole 2x2x4 slice. The times are simulated.
32 devices in a mesh: dp: 4 (over y, x), fsdp: 2 (over core), ctx: 4 (over z).
Axes of the slice: x: 2, y: 2, z: 4, core: 2. Of those that a mesh axis runs over, the one named last changes fastest.
Arguments:
- tokens: bfloat16 [16384, 8192], P(('dp', 'ctx')), may hold values from -6 to 6
- grad_hidden: bfloat16 [16384, 256], P(('dp', 'ctx'), 'fsdp'), may hold values from -0.0625 to 0.0625
- master: float32 [256, 8192], P(('fsdp', 'ctx')), may hold values from -3 to 3
- first_moment: float32 [256, 8192], P(('fsdp', 'ctx')), may hold values from -2 to 2
- second_moment: float32 [256, 8192], P(('fsdp', 'ctx')), may hold values from 0.01 to 1
- clip_scale: float32 [], replicated, may hold values from 0.2 to 1
Outputs:
- new_weights: bfloat16 [256, 8192], P('fsdp')
- new_master: float32 [256, 8192], P(('fsdp', 'ctx'))
- new_first: float32 [256, 8192], P(('fsdp', 'ctx'))
- new_second: float32 [256, 8192], P(('fsdp', 'ctx'))
All inputs are finite; a program needn't handle non-finite values.
Results may differ from a plain program's by a relative error of at most 0.005.
Values may be sent and summed in bfloat16 or wider, within the bound.
A program may use at most 128 MiB of HBM per device.

v0:
```python
import jax
import jax.numpy as jnp
from jax import lax
from jax.sharding import PartitionSpec as P

STEP = 10


BETA_ONE = 0.9
BETA_TWO = 0.95
EPSILON = 1e-08
LEARNING_RATE = 0.02
DECAY = 0.1


def contract(columns, tokens):
    return lax.dot_general(
        columns, tokens, (((0,), (0,)), ((), ())), preferred_element_type=jnp.float32
    )


def adamw(grad_sum, master, first_moment, second_moment, clip_scale):
    scaled = clip_scale * grad_sum
    first_new = BETA_ONE * first_moment + (1.0 - BETA_ONE) * scaled
    second_new = BETA_TWO * second_moment + (1.0 - BETA_TWO) * scaled * scaled
    first_hat = first_new / (1.0 - BETA_ONE**STEP)
    second_hat = second_new / (1.0 - BETA_TWO**STEP)
    update = first_hat / (jnp.sqrt(second_hat) + EPSILON)
    fresh_master = master - LEARNING_RATE * (update + DECAY * master)
    return (fresh_master, first_new, second_new)


def per_device(tokens, grad_hidden, master, first_moment, second_moment, clip_scale):
    ctx_count = lax.axis_size("ctx")
    dp_count = lax.axis_size("dp")
    row_dev = master.shape[0]
    width = tokens.shape[1]
    piece_rows = row_dev // dp_count
    tok_rows = grad_hidden.shape[0]
    reordered = (
        grad_hidden.reshape(tok_rows, ctx_count, dp_count, piece_rows)
        .transpose(0, 2, 1, 3)
        .reshape(tok_rows, ctx_count * dp_count * piece_rows)
    )
    partial_terms = contract(reordered, tokens).astype(jnp.bfloat16)
    piece_terms = partial_terms.reshape(dp_count * ctx_count, piece_rows, width)
    received = lax.all_to_all(piece_terms, ("dp", "ctx"), split_axis=0, concat_axis=0, tiled=True)
    piece_grad = jnp.sum(received, axis=0, dtype=jnp.float32)
    offset = lax.axis_index("dp") * piece_rows
    master_piece = lax.dynamic_slice_in_dim(master, offset, piece_rows, 0)
    first_piece = lax.dynamic_slice_in_dim(first_moment, offset, piece_rows, 0)
    second_piece = lax.dynamic_slice_in_dim(second_moment, offset, piece_rows, 0)
    fresh_piece, first_fresh, second_fresh = adamw(
        piece_grad, master_piece, first_piece, second_piece, clip_scale
    )
    new_master, new_first, new_second = (
        lax.all_gather(fresh_piece.astype(jnp.bfloat16), "dp", axis=0, tiled=True).astype(
            fresh_piece.dtype
        ),
        lax.all_gather(first_fresh.astype(jnp.bfloat16), "dp", axis=0, tiled=True).astype(
            first_fresh.dtype
        ),
        lax.all_gather(second_fresh.astype(jnp.bfloat16), "dp", axis=0, tiled=True).astype(
            second_fresh.dtype
        ),
    )
    new_weights = lax.all_gather(new_master.astype(jnp.bfloat16), "ctx", axis=0, tiled=True)
    return (new_weights, new_master, new_first, new_second)


def solution(mesh):
    in_specs = (
        P(("dp", "ctx"), None),
        P(("dp", "ctx"), "fsdp"),
        P(("fsdp", "ctx"), None),
        P(("fsdp", "ctx"), None),
        P(("fsdp", "ctx"), None),
        P(),
    )
    out_specs = (
        P("fsdp", None),
        P(("fsdp", "ctx"), None),
        P(("fsdp", "ctx"), None),
        P(("fsdp", "ctx"), None),
    )
    return jax.shard_map(
        per_device, mesh=mesh, in_specs=in_specs, out_specs=out_specs, check_vma=False
    )
```

profile of v0, /device:TPU:0, one launch (start us, length us, event | category | flops | bytes accessed | tf_op | source)
XLA Modules:
  0.0 141.5 jit_solution(3113973933799284460)
XLA Ops:
  7.2 1.1 copy.10
  8.3 9.5 %fusion = bf16[16,8,8192]{2,1,0:T(8,128)(2,1)} fusion(bf16[1024,128]{0,1:T(8,128)(2,1)S(1)} %bitcast.8, bf16[1024,8192]{1,0:T(8,128)(2,1)} %param.6), kind=kOutput, calls=%fused_computation.1 | convolution fusion | flops 2148532224 | bytes 19136512 | tf_op jit(solution)/shard_map/dot_general | solution.py:17
  17.7 8.3 %all-to-all-start = ((bf16[16,8,8192]{2,1,0:T(8,128)(2,1)}), bf16[16,8,8192]{2,1,0:T(8,128)(2,1)S(1)}, u32[]{:S(2)}, u32[]{:S(2)}) async-start(bf16[16,8,8192]{2,1,0:T(8,128)(2,1)} %fusion), calls=%async_computation | async-start | bytes 4194304 | tf_op jit(solution)/shard_map/all_to_all | solution.py:47
  26.1 0.0 all-gather.2.cloned.1.call-start
  26.8 49.2 %all-to-all-done = bf16[16,8,8192]{2,1,0:T(8,128)(2,1)S(1)} async-done(((bf16[16,8,8192]{2,1,0:T(8,128)(2,1)}), bf16[16,8,8192]{2,1,0:T(8,128)(2,1)S(1)}, u32[]{:S(2)}, u32[]{:S(2)}) %all-to-all-start) | async-done | bytes 2097184 | tf_op jit(solution)/shard_map/all_to_all | solution.py:47
  76.0 0.3 convert_reduce_fusion
  76.3 1.4 fusion.3
  77.7 9.8 %all_gather.12 = bf16[32,8192]{1,0:T(8,128)(2,1)} all-gather(bf16[8,8192]{1,0:T(8,128)(2,1)S(1)} %get-tuple-element.5), channel_id=1, replica_groups=mesh['dp'=4,'fsdp'=2,'ctx'=4] {'dp'}, dimensions={0}, use_global_device_ids=true | all-gather | bytes 655360 | tf_op jit(solution)/shard_map/all_gather | solution.py:57
  87.4 0.0 all-gather.2.cloned.1.call-update
  87.5 2.1 %convert_element_type.28 = f32[32,8192]{1,0:T(8,128)} convert(bf16[32,8192]{1,0:T(8,128)(2,1)} %all_gather.12) | non-fusion elementwise | flops 262144 | bytes 1572864 | tf_op jit(solution)/shard_map/convert_element_type | solution.py:57
  89.5 10.0 %all_gather.15 = bf16[32,8192]{1,0:T(8,128)(2,1)S(1)} all-gather(bf16[8,8192]{1,0:T(8,128)(2,1)S(1)} %get-tuple-element.4), channel_id=1, replica_groups=mesh['dp'=4,'fsdp'=2,'ctx'=4] {'dp'}, dimensions={0}, use_global_device_ids=true | all-gather | bytes 655360 | tf_op jit(solution)/shard_map/all_gather | solution.py:63
  99.5 1.0 convert_element_type.32
  100.6 9.3 %all_gather.14 = bf16[32,8192]{1,0:T(8,128)(2,1)S(1)} all-gather(bf16[8,8192]{1,0:T(8,128)(2,1)S(1)} %get-tuple-element.6), channel_id=1, replica_groups=mesh['dp'=4,'fsdp'=2,'ctx'=4] {'dp'}, dimensions={0}, use_global_device_ids=true | all-gather | bytes 655360 | tf_op jit(solution)/shard_map/all_gather | solution.py:60
  109.9 1.0 convert_element_type.30
  111.0 20.6 %all-gather.2.cloned.1.call-done = bf16[128,8192]{1,0:T(8,128)(2,1)} async-done(((bf16[32,8192]{1,0:T(8,128)(2,1)}), bf16[128,8192]{1,0:T(8,128)(2,1)}) %all-gather.2.cloned.1.call-update) | async-done | bytes 2097168 | tf_op jit(solution)/shard_map/all_gather | solution.py:67
  131.6 3.1 %copy.14 = bf16[128,8192]{1,0:T(8,128)(2,1)} copy(bf16[128,8192]{1,0:T(8,128)(2,1)} %all-gather.2.cloned.1.call-done) | data formatting | bytes 4194304
  (1 shorter events, 0.0 us)
Async XLA Ops:
  17.7 58.3 %all-to-all-start = ((bf16[16,8,8192]{2,1,0:T(8,128)(2,1)}), bf16[16,8,8192]{2,1,0:T(8,128)(2,1)S(1)}, u32[]{:S(2)}, u32[]{:S(2)}) async-start(bf16[16,8,8192]{2,1,0:T(8,128)(2,1)} %fusion), calls=%async_computation | async-start | bytes 4194304 | tf_op jit(solution)/shard_map/all_to_all | solution.py:47
  26.1 105.5 %all-gather.2.cloned.1.call-start = ((), (), s32[]{:S(2)}) async-start(), calls=%async_computation.1 | async-start | bytes 2621440 | tf_op jit(solution)/shard_map/all_gather | solution.py:67
Sparse Core Ops, SparseCore 0:
  87.6 43.9 all-gather.1
where the time goes:
time: 142 us
  waiting for transfers between devices  69.9 us (49%)
  blocking collectives  29.1 us (20%)
  between operations  14.7 us (10%)
  matrix products  9.45 us (7%)
  starting transfers between devices  8.35 us (6%)
  other arithmetic  5.81 us (4%)
  local copies, waits for them, and re-layouts  4.2 us (3%)
    all_to_all x1, waiting for transfers between devices, per_device(): lax.all_to_all(piece_terms, ('dp', 'ctx'), split_axis=0, concat_axis=0, t...  49.2 us
    all_gather x1, waiting for transfers between devices, per_device(): lax.all_gather(new_master.astype(jnp.bfloat16), 'ctx', axis=0, tiled=True)  20.6 us
    all_gather x1, blocking collectives, per_device(): lax.all_gather(second_fresh.astype(jnp.bfloat16), 'dp', axis=0, tiled=True)  10 us
    all_gather x1, blocking collectives, per_device(): lax.all_gather(fresh_piece.astype(jnp.bfloat16), 'dp', axis=0, tiled=True)  9.78 us
    dot_general x1, matrix products, contract(): lax.dot_general(columns, tokens, (((0,), (0,)), ((), ())), preferred_elem...  9.45 us
    all_gather x1, blocking collectives, per_device(): lax.all_gather(first_fresh.astype(jnp.bfloat16), 'dp', axis=0, tiled=True)  9.32 us
    all_to_all x1, starting transfers between devices, per_device(): lax.all_to_all(piece_terms, ('dp', 'ctx'), split_axis=0, concat_axis=0, t...  8.31 us
    unnamed x2, local copies, waits for them, and re-layouts  4.18 us
  transfers between devices with their start and end apart: 2, of which 2 were waited for; matrix products, arithmetic and copies ran while one was open for 3% of the time, Pallas kernels for 0%

commit v1 on v0

v1 whole, which is shorter than its diff:
```python
import functools

import jax
import jax.numpy as jnp
from jax import lax
from jax.experimental import pallas as pl
from jax.experimental.pallas import tpu as pltpu
from jax.sharding import PartitionSpec as P

STEP = 10


BETA_ONE = 0.9
BETA_TWO = 0.95
EPSILON = 1e-08
LEARNING_RATE = 0.02
DECAY = 0.1

CHUNKS = 8
MESH = pl.DeviceIdType.MESH


def adamw(grad_sum, master, first_moment, second_moment, clip_scale):
    scaled = clip_scale * grad_sum
    first_new = BETA_ONE * first_moment + (1.0 - BETA_ONE) * scaled
    second_new = BETA_TWO * second_moment + (1.0 - BETA_TWO) * scaled * scaled
    first_hat = first_new / (1.0 - BETA_ONE**STEP)
    second_hat = second_new / (1.0 - BETA_TWO**STEP)
    update = first_hat / (jnp.sqrt(second_hat) + EPSILON)
    fresh_master = master - LEARNING_RATE * (update + DECAY * master)
    return (fresh_master, first_new, second_new)


def kernel(
    nd, nc, piece, chunks,
    clip_ref, grad_ref, tok_hbm, master_hbm, first_hbm, second_hbm,
    sum_out, weight_out,
    columns, tok, master, first, second,
    part_send, part_recv, mid_send, mid_recv, sum_send, weights,
    tok_sem, state_sem, local_sem,
    part_ss, part_rs, mid_ss, mid_rs, sum_ss, sum_rs, near_ss, near_rs, far_ss, far_rs,
):
    d = lax.axis_index("dp")
    c = lax.axis_index("ctx")
    width = tok.shape[1] // chunks

    def cols(k):
        return pl.ds(pl.multiple_of(k * width, 128), width)

    def tok_copy(k):
        return pltpu.make_async_copy(tok_hbm.at[:, cols(k)], tok.at[:, cols(k)], tok_sem.at[k])

    def state_copies():
        rows = pl.ds(pl.multiple_of(d * piece, piece), piece)
        return [
            pltpu.make_async_copy(src.at[rows], dst, state_sem.at[i])
            for i, (src, dst) in enumerate(
                ((master_hbm, master), (first_hbm, first), (second_hbm, second))
            )
        ]

    def local_copies(k):
        return [
            pltpu.make_async_copy(sum_send.at[k], sum_out.at[d, :, cols(k)], local_sem.at[0, k]),
            pltpu.make_async_copy(weights.at[k], weight_out.at[:, d, :, cols(k)], local_sem.at[1, k]),
        ]

    def send(src, dst, ss, rs, axis, target):
        pltpu.make_async_remote_copy(
            src_ref=src, dst_ref=dst, send_sem=ss, recv_sem=rs,
            device_id={axis: target}, device_id_type=MESH,
        ).start()

    def take(like, sem):
        pltpu.make_async_copy(like, like, sem).wait()

    @pl.loop(0, chunks)
    def _(k):
        tok_copy(k).start()

    for copy in state_copies():
        copy.start()

    barrier = pltpu.get_barrier_semaphore()
    for j in range(1, nd):
        pl.semaphore_signal(
            barrier, inc=1, device_id={"dp": lax.rem(d + j, nd)}, device_id_type=MESH
        )
    for j in range(1, nc):
        pl.semaphore_signal(
            barrier, inc=1, device_id={"ctx": lax.rem(c + j, nc)}, device_id_type=MESH
        )
    columns[...] = grad_ref[...].T
    pl.semaphore_wait(barrier, nd + nc - 2)

    @pl.loop(0, chunks)
    def _(k):
        tok_copy(k).wait()
        partial = jnp.dot(columns[...], tok[:, cols(k)], preferred_element_type=jnp.float32)
        partial = partial.reshape(nc, nd, piece, width)
        for e in range(nd):
            part_send[k, e] = partial[:, e].astype(jnp.bfloat16)
        for j in range(1, nd):
            to = lax.rem(d + j, nd)
            send(
                part_send.at[k, to], part_recv.at[k, j - 1], part_ss.at[k], part_rs.at[k], "dp", to
            )

    for copy in state_copies():
        copy.wait()

    @pl.loop(0, chunks + 2)
    def _(t):
        @pl.when(t < chunks)
        def _():
            k = t
            take(part_recv.at[k], part_rs.at[k])
            total = part_send[k, d].astype(jnp.float32)
            for j in range(nd - 1):
                total = total + part_recv[k, j].astype(jnp.float32)
            mid_send[k] = total.astype(jnp.bfloat16)
            for j in range(1, nc):
                to = lax.rem(c + j, nc)
                send(
                    mid_send.at[k, to], mid_recv.at[k, j - 1], mid_ss.at[k], mid_rs.at[k], "ctx", to
                )

        @pl.when(jnp.logical_and(t >= 1, t < chunks + 1))
        def _():
            k = t - 1
            take(mid_recv.at[k], mid_rs.at[k])
            total = mid_send[k, c].astype(jnp.float32)
            for j in range(nc - 1):
                total = total + mid_recv[k, j].astype(jnp.float32)
            rounded = total.astype(jnp.bfloat16)
            sum_send[k] = rounded
            fresh, _, _ = adamw(
                rounded.astype(jnp.float32),
                master[:, cols(k)], first[:, cols(k)], second[:, cols(k)], clip_ref[0],
            )
            weights[k, c] = fresh.astype(jnp.bfloat16)
            for j in range(1, nc):
                send(
                    weights.at[k, c], weights.at[k, c], near_ss.at[k], near_rs.at[k],
                    "ctx", lax.rem(c + j, nc),
                )
            for j in range(1, nd):
                send(
                    sum_send.at[k], sum_out.at[d, :, cols(k)], sum_ss.at[k], sum_rs.at[k],
                    "dp", lax.rem(d + j, nd),
                )

        @pl.when(t >= 2)
        def _():
            k = t - 2
            take(mid_recv.at[k], near_rs.at[k])
            for j in range(1, nd):
                send(
                    weights.at[k], weight_out.at[:, d, :, cols(k)], far_ss.at[k], far_rs.at[k],
                    "dp", lax.rem(d + j, nd),
                )
            for copy in local_copies(k):
                copy.start()

    @pl.loop(0, chunks)
    def _(k):
        for copy in local_copies(k):
            copy.wait()
        take(part_recv.at[k], part_ss.at[k])
        take(mid_recv.at[k], mid_ss.at[k])
        take(mid_recv.at[k], near_ss.at[k])
        take(part_recv.at[k, :, 0], sum_ss.at[k])
        take(part_recv.at[k, :, 0], sum_rs.at[k])
        take(part_recv.at[k], far_ss.at[k])
        take(part_recv.at[k], far_rs.at[k])


def per_device(tokens, grad_hidden, master, first_moment, second_moment, clip_scale):
    nc = lax.axis_size("ctx")
    nd = lax.axis_size("dp")
    row_dev, dim = master.shape
    piece = row_dev // nd
    tok_rows, rows = grad_hidden.shape
    width = dim // CHUNKS
    bf16, f32 = jnp.bfloat16, jnp.float32
    dma = pltpu.SemaphoreType.DMA
    hbm = pl.BlockSpec(memory_space=pl.ANY)
    grad_sum, weights = pl.pallas_call(
        functools.partial(kernel, nd, nc, piece, CHUNKS),
        out_shape=(
            jax.ShapeDtypeStruct((nd, piece, dim), bf16),
            jax.ShapeDtypeStruct((nc, nd, piece, dim), bf16),
        ),
        in_specs=[
            pl.BlockSpec(memory_space=pltpu.SMEM),
            pl.BlockSpec(memory_space=pltpu.VMEM),
            hbm, hbm, hbm, hbm,
        ],
        out_specs=(hbm, hbm),
        scratch_shapes=[
            pltpu.VMEM((rows, tok_rows), bf16),
            pltpu.VMEM((tok_rows, dim), bf16),
            pltpu.VMEM((piece, dim), f32),
            pltpu.VMEM((piece, dim), f32),
            pltpu.VMEM((piece, dim), f32),
            pltpu.VMEM((CHUNKS, nd, nc, piece, width), bf16),
            pltpu.VMEM((CHUNKS, nd - 1, nc, piece, width), bf16),
            pltpu.VMEM((CHUNKS, nc, piece, width), bf16),
            pltpu.VMEM((CHUNKS, nc - 1, piece, width), bf16),
            pltpu.VMEM((CHUNKS, piece, width), bf16),
            pltpu.VMEM((CHUNKS, nc, piece, width), bf16),
            dma((CHUNKS,)), dma((3,)), dma((2, CHUNKS)),
        ] + [dma((CHUNKS,))] * 10,
        compiler_params=pltpu.CompilerParams(
            collective_id=0, has_side_effects=True, vmem_limit_bytes=56 << 20
        ),
        cost_estimate=pl.CostEstimate(
            flops=2 * rows * tok_rows * dim,
            bytes_accessed=2 * tok_rows * dim + 4 * rows * dim,
            transcendentals=0,
        ),
    )(clip_scale.reshape(1), grad_hidden, tokens, master, first_moment, second_moment)
    new_master, new_first, new_second = adamw(
        grad_sum.reshape(row_dev, dim).astype(f32), master, first_moment, second_moment, clip_scale
    )
    return (weights.reshape(rows, dim), new_master, new_first, new_second)


def solution(mesh):
    in_specs = (
        P(("dp", "ctx"), None),
        P(("dp", "ctx"), "fsdp"),
        P(("fsdp", "ctx"), None),
        P(("fsdp", "ctx"), None),
        P(("fsdp", "ctx"), None),
        P(),
    )
    out_specs = (
        P("fsdp", None),
        P(("fsdp", "ctx"), None),
        P(("fsdp", "ctx"), None),
        P(("fsdp", "ctx"), None),
    )
    return jax.shard_map(
        per_device, mesh=mesh, in_specs=in_specs, out_specs=out_specs, check_vma=False
    )
```

time: 142 us -> 66.7 us (0.47)
  waiting for transfers between devices: 69.9 us -> 0 us
  Pallas kernels: 0 us -> 60.4 us
  blocking collectives: 29.1 us -> 0 us
  between operations: 14.7 us -> 1.34 us
  matrix products: 9.45 us -> 0 us
  starting transfers between devices: 8.35 us -> 0 us
  local copies, waits for them, and re-layouts: 4.2 us -> 1.34 us
  other arithmetic: 5.81 us -> 3.38 us
    pallas_call x0 -> x1, Pallas kernels: none -> 60.4 us  [per_device(): pl.pallas_call(functools.partial(kernel, nd, nc, piece, CHUNKS), out_shap...]
    all_to_all x1 -> x0, waiting for transfers between devices: 49.2 us -> none  [per_device(): lax.all_to_all(piece_terms, ('dp', 'ctx'), split_axis=0, concat_axis=0, t...]
    all_gather x3 -> x0, blocking collectives: 29.1 us -> none  [the longest x1 10 us: per_device(): lax.all_gather(second_fresh.astype(jnp.bfloat16), 'dp', axis=0, tiled=True)]
    all_gather x1 -> x0, waiting for transfers between devices: 20.6 us -> none  [per_device(): lax.all_gather(new_master.astype(jnp.bfloat16), 'ctx', axis=0, tiled=True)]
    dot_general x1 -> x0, matrix products: 9.45 us -> none  [contract(): lax.dot_general(columns, tokens, (((0,), (0,)), ((), ())), preferred_elem...]
    all_to_all x1 -> x0, starting transfers between devices: 8.31 us -> none  [per_device(): lax.all_to_all(piece_terms, ('dp', 'ctx'), split_axis=0, concat_axis=0, t...]
    convert_element_type x4 -> x0, other arithmetic: 5.52 us -> none  [the longest x1 2.08 us: per_device(): lax.all_gather(fresh_piece.astype(jnp.bfloat16), 'dp', axis=0, tiled=True)]
    sub x0 -> x1, other arithmetic: none -> 3.38 us  [adamw(): fresh_master = master - LEARNING_RATE * (update + DECAY * master)]
  transfers between devices with their start and end apart: 2 -> 0, of which waited for: 2 -> 0; matrix products, arithmetic and copies ran while one was open for 3% -> 0% of each run, Pallas kernels for 0% -> 0%
where the time goes in v1:
time: 66.7 us; the launch traced here: 66.5 us
  Pallas kernels  60.4 us (91%)
  other arithmetic  3.38 us (5%)
  local copies, waits for them, and re-layouts  1.34 us (2%)
  between operations  1.34 us (2%)
    pallas_call x1, Pallas kernels, per_device(): pl.pallas_call(functools.partial(kernel, nd, nc, piece, CHUNKS), out_shap...  60.4 us
    sub x1, other arithmetic, adamw(): fresh_master = master - LEARNING_RATE * (update + DECAY * master)  3.38 us
    unnamed x9, local copies, waits for them, and re-layouts  1.34 us

profile of v1, /device:TPU:0, one launch (start us, length us, event | category | flops | bytes accessed | tf_op | source)
XLA Modules:
  0.0 66.5 jit_solution(12731414384411476760)
XLA Ops:
  1.3 0.0 copy-start
  1.3 0.0 copy-start.1
  1.3 0.0 copy-start.2
  1.3 60.4 %shard_map.93 = (bf16[4,8,8192]{2,1,0:T(8,128)(2,1)}, bf16[4,4,8,8192]{3,2,1,0:T(8,128)(2,1)}) custom-call(f32[1]{0:T(128)} %bitcast.9.clip_ref, bf16[1024,128]{1,0:T(8,128)(2,1)} %grad_ref.1, bf16[1024,8192]{1,0:T(8,128)(2,1)} %tok_hbm.1, f32[32,8192]{1,0:T(8,128)} %master_hbm.1, f32[32,8192]{1,0:T(8,128)} %first_hbm.1, f32[32,8192]{1,0:T(8,128)} %second_hbm.1), custom_call_target="tpu_custom_call" | custom-call | flops 2147483648 | bytes 20971520 | tf_op jit(solution)/shard_map/pallas_call | solution.py:188
  61.8 0.0 copy-done
  61.8 0.0 copy-done.1
  61.8 0.0 copy-done.2
  61.8 0.0 copy-start.3
  61.8 3.4 %multiply_subtract_fusion = (f32[32,8192]{1,0:T(8,128)}, f32[32,8192]{1,0:T(8,128)}, f32[32,8192]{1,0:T(8,128)}) fusion(f32[32,8192]{1,0:T(8,128)S(1)} %copy-done, bf16[4,8,8192]{2,1,0:T(8,128)(2,1)} %get-tuple-element.7, f32[]{:T(128)} %copy.11, f32[32,8192]{1,0:T(8,128)S(1)} %copy-done.1, f32[32,8192]{1,0:T(8,128)S(1)} %copy-done.2), kind=kLoop, calls=%fused_computation.4 | loop fusion | flops 4456448 | bytes 6815748 | tf_op jit(solution)/shard_map/sub | solution.py:30
  65.2 0.0 copy-done.3
  65.2 1.3 %copy.12 = bf16[128,8192]{1,0:T(8,128)(2,1)} copy(bf16[128,8192]{1,0:T(8,128)(2,1)S(1)} %bitcast.10) | data formatting | bytes 4194304
Async XLA Ops:
  1.3 60.5 %copy-start = (f32[32,8192]{1,0:T(8,128)S(1)}, f32[32,8192]{1,0:T(8,128)}, u32[]{:S(2)}) copy-start(f32[32,8192]{1,0:T(8,128)} %master_hbm.1) | copy-start | bytes 3145732
  1.3 60.5 %copy-start.1 = (f32[32,8192]{1,0:T(8,128)S(1)}, f32[32,8192]{1,0:T(8,128)}, u32[]{:S(2)}) copy-start(f32[32,8192]{1,0:T(8,128)} %first_hbm.1) | copy-start | bytes 3145732
  1.3 60.5 %copy-start.2 = (f32[32,8192]{1,0:T(8,128)S(1)}, f32[32,8192]{1,0:T(8,128)}, u32[]{:S(2)}) copy-start(f32[32,8192]{1,0:T(8,128)} %second_hbm.1) | copy-start | bytes 3145732
  61.8 3.4 %copy-start.3 = (bf16[4,4,8,8192]{3,2,1,0:T(8,128)(2,1)S(1)}, bf16[4,4,8,8192]{3,2,1,0:T(8,128)(2,1)}, u32[]{:S(2)}) copy-start(bf16[4,4,8,8192]{3,2,1,0:T(8,128)(2,1)} %get-tuple-element.6) | copy-start | bytes 6291460
